TPU v7x, 32 devices: a whole 2x2x4 slice. The times are simulated.
32 devices in a mesh: ctx: 8 (over y, x, core), fsdp: 4 (over z).
Axes of the slice: x: 2, y: 2, z: 4, core: 2. Of those that a mesh axis runs over, the one named last changes fastest.
Arguments:
- tokens: bfloat16 [4, 1024, 2048], P('fsdp', 'ctx'), may hold values from -6 to 6
- cotangent: bfloat16 [4, 1024, 2048], P('fsdp', 'ctx'), may hold values from -6 to 6
- pairing: int32 [8, 2], replicated, may hold values from 0 to 15, as said below
- norm_attn: float32 [2048], P('fsdp'), may hold values from 0.5 to 1.5
- w_query: bfloat16 [2048, 2048], P('fsdp'), may hold values from -0.125 to 0.125
- w_key: bfloat16 [2048, 512], P('fsdp'), may hold values from -0.125 to 0.125
- w_value: bfloat16 [2048, 512], P('fsdp'), may hold values from -0.125 to 0.125
- w_out: bfloat16 [2048, 2048], P('fsdp'), may hold values from -0.5 to 0.5
- norm_mlp: float32 [2048], P('fsdp'), may hold values from 0.5 to 1.5
- w_gate: bfloat16 [2048, 8192], P('fsdp'), may hold values from -0.125 to 0.125
- w_up: bfloat16 [2048, 8192], P('fsdp'), may hold values from -0.125 to 0.125
- w_down: bfloat16 [8192, 2048], P('fsdp'), may hold values from -0.0625 to 0.0625
Outputs:
- output: bfloat16 [4, 1024, 2048], P('fsdp', 'ctx')
- d_tokens: bfloat16 [4, 1024, 2048], P('fsdp', 'ctx')
- grad_norm_attn: float32 [2048], P('fsdp')
- grad_query: float32 [2048, 2048], P('fsdp')
- grad_key: float32 [2048, 512], P('fsdp')
- grad_value: float32 [2048, 512], P('fsdp')
- grad_out: float32 [2048, 2048], P('fsdp')
- grad_norm_mlp: float32 [2048], P('fsdp')
- grad_gate: float32 [2048, 8192], P('fsdp')
- grad_up: float32 [2048, 8192], P('fsdp')
- grad_down: float32 [8192, 2048], P('fsdp')
Inputs may be any that keep to these rules, and one draw needn't show every extreme that they name: `pairing`: each of the 16 block numbers appears exactly once; each row holds a block number b and its mirror 16 - 1 - b, in either order.
All inputs are finite; a program needn't handle non-finite values.
Results may differ from a plain program's by a relative error of at most 0.035.
Values may be sent and summed in bfloat16 or wider, within the bound.
A program may use at most 448 MiB of HBM per device.

v0:
```python
import math
import jax
import jax.numpy as jnp
from jax import lax
from jax.sharding import PartitionSpec as P

HEAD_DIM = 64
KBLK = 512
EPS = 1e-05
THETA = 500000.0


def frequencies(head_width):
    evens = jnp.arange(0, head_width, 2, dtype=jnp.float32)
    inverse = 1.0 / THETA ** (evens / head_width)
    wavelen = 2.0 * math.pi / inverse
    smooth = (8192.0 / wavelen - 1.0) / 3.0
    middle = (1.0 - smooth) * inverse / 32.0 + smooth * inverse
    return jnp.where(wavelen < 2048.0, inverse, jnp.where(wavelen > 8192.0, inverse / 32.0, middle))


def rotation(positions, head_width):
    angles = positions.astype(jnp.float32)[:, None] * frequencies(head_width)[None, :]
    cosine = jnp.concatenate([jnp.cos(angles), jnp.cos(angles)], axis=1)[:, None, :]
    sine = jnp.concatenate([jnp.sin(angles), jnp.sin(angles)], axis=1)[:, None, :]
    return (cosine, sine)


def rotate(tensor, cosine, sine):
    middle = tensor.shape[-1] // 2
    turned = jnp.concatenate([-tensor[..., middle:], tensor[..., :middle]], axis=-1)
    return tensor * cosine + turned * sine


def unrotate(gradient, cosine, sine):
    middle = gradient.shape[-1] // 2
    moved = gradient * sine
    back_turn = jnp.concatenate([moved[..., middle:], -moved[..., :middle]], axis=-1)
    return gradient * cosine + back_turn


def slot_positions(pairing, seq_length, block_len):
    flattened = pairing.reshape(-1)
    slots = jnp.arange(seq_length, dtype=jnp.int32)
    owning = slots // block_len
    labels = jnp.arange(flattened.shape[0], dtype=jnp.int32)
    anchor = jnp.sum(jnp.where(owning[:, None] == labels[None, :], flattened[None, :], 0), axis=1)
    return anchor * block_len + slots % block_len


def product(left, right):
    return jnp.dot(left, right, preferred_element_type=jnp.float32)


def product_t(left, right):
    return lax.dot_general(
        left, right, (((1,), (1,)), ((), ())), preferred_element_type=jnp.float32
    )


def tokens_t(left, right):
    return lax.dot_general(
        left, right, (((0,), (0,)), ((), ())), preferred_element_type=jnp.float32
    )


def own_columns(matrix, rows):
    return lax.dynamic_slice_in_dim(matrix, lax.axis_index("fsdp") * rows, rows, 1)


def pair_fold(totals, pieces):
    first_rows = totals[0].shape[0]
    second_rows = totals[1].shape[0]
    first = tokens_t(own_columns(pieces[0], first_rows), pieces[1])
    second = tokens_t(own_columns(pieces[2], second_rows), pieces[3])
    return (first, second)


def norm_back(upstream, gain, unit, scale):
    weighted = upstream * gain
    return scale * (weighted - unit * jnp.mean(weighted * unit, axis=1, keepdims=True))


def on_device(
    tokens,
    cotangent,
    pairing,
    norm_attn,
    w_query,
    w_key,
    w_value,
    w_out,
    norm_mlp,
    w_gate,
    w_up,
    w_down,
):
    inputs = tokens[0].astype(jnp.float32)
    tok_rows = inputs.shape[0]
    seq_length = tok_rows * lax.axis_size("ctx")
    heads_kv = w_key.shape[1] // HEAD_DIM
    group_size = w_query.shape[1] // w_key.shape[1]
    all_pos = slot_positions(pairing, seq_length, tok_rows // 2)
    own_pos = lax.dynamic_slice_in_dim(all_pos, lax.axis_index("ctx") * tok_rows, tok_rows)
    cosine, sine = rotation(own_pos, HEAD_DIM)
    factor = HEAD_DIM ** (-0.5)
    gain_attn, query_full, key_full, value_full, out_full = (
        lax.all_gather(norm_attn.astype(jnp.bfloat16), "fsdp", axis=0, tiled=True).astype(
            norm_attn.dtype
        ),
        lax.all_gather(w_query, "fsdp", axis=0, tiled=True),
        lax.all_gather(w_key, "fsdp", axis=0, tiled=True),
        lax.all_gather(w_value, "fsdp", axis=0, tiled=True),
        lax.all_gather(w_out, "fsdp", axis=0, tiled=True),
    )
    scale_attn = lax.rsqrt(jnp.mean(inputs * inputs, axis=1, keepdims=True) + EPS)
    unit_attn = inputs * scale_attn
    normed_attn = (unit_attn * gain_attn).astype(jnp.bfloat16)
    query_rot = rotate(
        product(normed_attn, query_full).reshape(tok_rows, -1, HEAD_DIM), cosine, sine
    )
    queries = query_rot.astype(jnp.bfloat16).reshape(tok_rows, heads_kv, group_size, HEAD_DIM)
    key_rot = rotate(
        product(normed_attn, key_full).reshape(tok_rows, heads_kv, HEAD_DIM), cosine, sine
    )
    keys_local = key_rot.astype(jnp.bfloat16).reshape(tok_rows, heads_kv * HEAD_DIM)
    values_local = product(normed_attn, value_full).astype(jnp.bfloat16)
    keys_all, values_all = (
        lax.all_gather(keys_local, "ctx", axis=0, tiled=True),
        lax.all_gather(values_local, "ctx", axis=0, tiled=True),
    )
    block_count = seq_length // KBLK
    key_blocks = keys_all.reshape(block_count, KBLK, heads_kv, HEAD_DIM)
    value_blocks = values_all.reshape(block_count, KBLK, heads_kv, HEAD_DIM)
    pos_blocks = all_pos.reshape(block_count, KBLK)

    def scores(key_blk, pos_blk):
        logits = jnp.einsum("qhgd,khd->hgqk", queries, key_blk, preferred_element_type=jnp.float32)
        allowed = pos_blk[None, :] <= own_pos[:, None]
        return (jnp.where(allowed, logits * factor, -1e30), allowed)

    def statistics(carry, item):
        running, total = carry
        score_blk, allowed = scores(item[0], item[1])
        newest = jnp.maximum(running, jnp.max(score_blk, axis=-1))
        added = jnp.sum(jnp.where(allowed, jnp.exp(score_blk - newest[..., None]), 0.0), axis=-1)
        return ((newest, total * jnp.exp(running - newest) + added), None)

    start_top = jnp.full((heads_kv, group_size, tok_rows), -1e30, jnp.float32)
    start_sum = jnp.zeros((heads_kv, group_size, tok_rows), jnp.float32)
    (running, total), _ = lax.scan(statistics, (start_top, start_sum), (key_blocks, pos_blocks))
    log_total = running + jnp.log(total)

    def weights_of(score_blk, allowed):
        return jnp.where(allowed, jnp.exp(score_blk - log_total[..., None]), 0.0)

    def attend(acc, item):
        key_blk, value_blk, pos_blk = item
        score_blk, allowed = scores(key_blk, pos_blk)
        probs_low = weights_of(score_blk, allowed).astype(jnp.bfloat16)
        return (
            acc
            + jnp.einsum(
                "hgqk,khd->qhgd", probs_low, value_blk, preferred_element_type=jnp.float32
            ),
            None,
        )

    start_acc = jnp.zeros((tok_rows, heads_kv, group_size, HEAD_DIM), jnp.float32)
    attended, _ = lax.scan(attend, start_acc, (key_blocks, value_blocks, pos_blocks))
    attended_low = attended.reshape(tok_rows, -1).astype(jnp.bfloat16)
    resid = inputs + product(attended_low, out_full)
    gain_mlp, gate_full, up_full, down_full = (
        lax.all_gather(norm_mlp.astype(jnp.bfloat16), "fsdp", axis=0, tiled=True).astype(
            norm_mlp.dtype
        ),
        lax.all_gather(w_gate, "fsdp", axis=0, tiled=True),
        lax.all_gather(w_up, "fsdp", axis=0, tiled=True),
        lax.all_gather(w_down, "fsdp", axis=0, tiled=True),
    )
    scale_mlp = lax.rsqrt(jnp.mean(resid * resid, axis=1, keepdims=True) + EPS)
    unit_mlp = resid * scale_mlp
    normed_mlp = (unit_mlp * gain_mlp).astype(jnp.bfloat16)
    gate_pre = product(normed_mlp, gate_full)
    up_pre = product(normed_mlp, up_full)
    sigma = jax.nn.sigmoid(gate_pre)
    swish = gate_pre * sigma
    hidden = (swish * up_pre).astype(jnp.bfloat16)
    output = resid + product(hidden, down_full)
    upstream = cotangent[0]
    gain_mlp, gate_full, up_full, down_full = (
        lax.all_gather(norm_mlp.astype(jnp.bfloat16), "fsdp", axis=0, tiled=True).astype(
            norm_mlp.dtype
        ),
        lax.all_gather(w_gate, "fsdp", axis=0, tiled=True),
        lax.all_gather(w_up, "fsdp", axis=0, tiled=True),
        lax.all_gather(w_down, "fsdp", axis=0, tiled=True),
    )
    d_hidden = product_t(upstream, down_full)
    d_gate = (d_hidden * up_pre * sigma * (1.0 + gate_pre * (1.0 - sigma))).astype(jnp.bfloat16)
    d_up = (d_hidden * swish).astype(jnp.bfloat16)
    d_normed_mlp = product_t(d_gate, gate_full) + product_t(d_up, up_full)
    gate_up_pair = jnp.concatenate([d_gate, d_up], axis=1)
    ff_width = w_gate.shape[1]
    down_rows = w_down.shape[0]
    model_rows = w_gate.shape[0]
    start_down = jnp.zeros((down_rows, upstream.shape[1]), jnp.float32)
    start_pair = jnp.zeros((model_rows, gate_up_pair.shape[1]), jnp.float32)
    grad_down, grad_pair = pair_fold(
        (start_down, start_pair),
        (
            lax.all_gather(hidden, "fsdp", axis=0, tiled=True),
            lax.all_gather(upstream, "fsdp", axis=0, tiled=True),
            lax.all_gather(normed_mlp, "fsdp", axis=0, tiled=True),
            lax.all_gather(gate_up_pair, "fsdp", axis=0, tiled=True),
        ),
    )
    grad_gate = grad_pair[:, :ff_width]
    grad_up = grad_pair[:, ff_width:]
    gain_mlp_term = jnp.sum(d_normed_mlp * unit_mlp, axis=0)
    d_resid = upstream.astype(jnp.float32) + norm_back(d_normed_mlp, gain_mlp, unit_mlp, scale_mlp)
    d_resid_low = d_resid.astype(jnp.bfloat16)
    gain_attn, query_full, key_full, value_full, out_full = (
        lax.all_gather(norm_attn.astype(jnp.bfloat16), "fsdp", axis=0, tiled=True).astype(
            norm_attn.dtype
        ),
        lax.all_gather(w_query, "fsdp", axis=0, tiled=True),
        lax.all_gather(w_key, "fsdp", axis=0, tiled=True),
        lax.all_gather(w_value, "fsdp", axis=0, tiled=True),
        lax.all_gather(w_out, "fsdp", axis=0, tiled=True),
    )
    d_attended = (
        product_t(d_resid_low, out_full)
        .astype(jnp.bfloat16)
        .reshape(tok_rows, heads_kv, group_size, HEAD_DIM)
    )
    delta = jnp.einsum("qhgd,qhgd->hgq", d_attended.astype(jnp.float32), attended)

    def backward_step(carry, item):
        key_blk, value_blk, pos_blk = item
        score_blk, allowed = scores(key_blk, pos_blk)
        probs = weights_of(score_blk, allowed)
        grad_val = jnp.einsum(
            "hgqk,qhgd->khd",
            probs.astype(jnp.bfloat16),
            d_attended,
            preferred_element_type=jnp.float32,
        )
        d_probs = jnp.einsum(
            "qhgd,khd->hgqk", d_attended, value_blk, preferred_element_type=jnp.float32
        )
        d_score = (probs * (d_probs - delta[..., None]) * factor).astype(jnp.bfloat16)
        carry = carry + jnp.einsum(
            "hgqk,khd->qhgd", d_score, key_blk, preferred_element_type=jnp.float32
        )
        grad_keyblk = jnp.einsum(
            "hgqk,qhgd->khd", d_score, queries, preferred_element_type=jnp.float32
        )
        return (carry, (grad_keyblk, grad_val))

    d_query_rot, (key_terms, value_terms) = lax.scan(
        backward_step, start_acc, (key_blocks, value_blocks, pos_blocks)
    )
    key_sum, value_sum = (
        lax.psum_scatter(
            key_terms.reshape(seq_length, -1).astype(jnp.bfloat16),
            "ctx",
            scatter_dimension=0,
            tiled=True,
        ).astype(jnp.float32),
        lax.psum_scatter(
            value_terms.reshape(seq_length, -1).astype(jnp.bfloat16),
            "ctx",
            scatter_dimension=0,
            tiled=True,
        ).astype(jnp.float32),
    )
    d_query = (
        unrotate(d_query_rot.reshape(tok_rows, -1, HEAD_DIM), cosine, sine)
        .reshape(tok_rows, -1)
        .astype(jnp.bfloat16)
    )
    d_key = (
        unrotate(key_sum.reshape(tok_rows, heads_kv, HEAD_DIM), cosine, sine)
        .reshape(tok_rows, -1)
        .astype(jnp.bfloat16)
    )
    d_value_low = value_sum.astype(jnp.bfloat16)
    d_normed_attn = (
        product_t(d_query, query_full)
        + product_t(d_key, key_full)
        + product_t(d_value_low, value_full)
    )
    joined = jnp.concatenate([d_query, d_key, d_value_low], axis=1)
    out_rows = w_out.shape[0]
    query_rows = w_query.shape[0]
    start_out = jnp.zeros((out_rows, d_resid_low.shape[1]), jnp.float32)
    start_joined = jnp.zeros((query_rows, joined.shape[1]), jnp.float32)
    grad_out, grad_joined = pair_fold(
        (start_out, start_joined),
        (
            lax.all_gather(attended_low, "fsdp", axis=0, tiled=True),
            lax.all_gather(d_resid_low, "fsdp", axis=0, tiled=True),
            lax.all_gather(normed_attn, "fsdp", axis=0, tiled=True),
            lax.all_gather(joined, "fsdp", axis=0, tiled=True),
        ),
    )
    query_width = w_query.shape[1]
    key_width = w_key.shape[1]
    grad_query = grad_joined[:, :query_width]
    grad_key = grad_joined[:, query_width : query_width + key_width]
    grad_value = grad_joined[:, query_width + key_width :]
    gain_attn_term = jnp.sum(d_normed_attn * unit_attn, axis=0)
    d_inputs = d_resid + norm_back(d_normed_attn, gain_attn, unit_attn, scale_attn)
    gain_attn_part, gain_mlp_part = (
        lax.psum_scatter(gain_attn_term, "fsdp", scatter_dimension=0, tiled=True),
        lax.psum_scatter(gain_mlp_term, "fsdp", scatter_dimension=0, tiled=True),
    )
    summed = (
        lax.psum(gain_attn_part.astype(jnp.bfloat16), "ctx").astype(jnp.float32),
        lax.psum(grad_query.astype(jnp.bfloat16), "ctx").astype(jnp.float32),
        lax.psum(grad_key.astype(jnp.bfloat16), "ctx").astype(jnp.float32),
        lax.psum(grad_value.astype(jnp.bfloat16), "ctx").astype(jnp.float32),
        lax.psum(grad_out.astype(jnp.bfloat16), "ctx").astype(jnp.float32),
        lax.psum(gain_mlp_part.astype(jnp.bfloat16), "ctx").astype(jnp.float32),
        lax.psum(grad_gate.astype(jnp.bfloat16), "ctx").astype(jnp.float32),
        lax.psum(grad_up.astype(jnp.bfloat16), "ctx").astype(jnp.float32),
        lax.psum(grad_down.astype(jnp.bfloat16), "ctx").astype(jnp.float32),
    )
    return (
        output.astype(jnp.bfloat16)[None],
        d_inputs.astype(jnp.bfloat16)[None],
        summed[0],
        summed[1],
        summed[2],
        summed[3],
        summed[4],
        summed[5],
        summed[6],
        summed[7],
        summed[8],
    )


def solution(mesh):
    return jax.shard_map(
        on_device,
        mesh=mesh,
        in_specs=(
            P("fsdp", "ctx", None),
            P("fsdp", "ctx", None),
            P(),
            P("fsdp"),
            P("fsdp", None),
            P("fsdp", None),
            P("fsdp", None),
            P("fsdp", None),
            P("fsdp"),
            P("fsdp", None),
            P("fsdp", None),
            P("fsdp", None),
        ),
        out_specs=(
            P("fsdp", "ctx", None),
            P("fsdp", "ctx", None),
            P("fsdp"),
            P("fsdp", None),
            P("fsdp", None),
            P("fsdp", None),
            P("fsdp", None),
            P("fsdp"),
            P("fsdp", None),
            P("fsdp", None),
            P("fsdp", None),
        ),
        check_vma=False,
    )
```

profile of v0, /device:TPU:0, one launch (start us, length us, event | category | flops | bytes accessed | tf_op | source)
XLA Modules:
  0.0 3507.1 jit_solution(8441512161050424623)
XLA Ops:
  9.4 13.5 all-gather.1
  25.5 32.8 all-gather.21.cloned.1.call-done
  62.3 42.2 %all-gather.25.cloned.1.call-done = bf16[2048,512]{1,0:T(8,128)(2,1)} async-done(((bf16[512,512]{1,0:T(8,128)(2,1)}), bf16[2048,512]{1,0:T(8,128)(2,1)}) %all-gather.25.cloned.1.call-update) | async-done | bytes 2097168 | tf_op jit(solution)/shard_map/all_gather | solution.py:112
  112.6 12.2 all-gather.2
  136.4 18.7 all-gather.27.cloned.1.call-done
  159.2 147.0 %all-gather.29.cloned.1.call-done = bf16[2048,2048]{1,0:T(8,128)(2,1)} async-done(((bf16[512,2048]{1,0:T(8,128)(2,1)}), bf16[2048,2048]{1,0:T(8,128)(2,1)}) %all-gather.29.cloned.1.call-update) | async-done | bytes 8388624 | tf_op jit(solution)/shard_map/all_gather | solution.py:111
  306.2 12.4 copy.73
  318.6 6.0 fusion.98
  324.9 19.0 while.39
  325.1 4.7 fusion.186
  334.6 4.7 fusion.186
  344.0 10.5 while.40
  349.0 5.0 fusion.192
  356.6 98.9 %all-gather.31.cloned.1.call-done = bf16[2048,2048]{1,0:T(8,128)(2,1)} async-done(((bf16[512,2048]{1,0:T(8,128)(2,1)}), bf16[2048,2048]{1,0:T(8,128)(2,1)}) %all-gather.31.cloned.1.call-update) | async-done | bytes 8388624 | tf_op jit(solution)/shard_map/all_gather | solution.py:114
  455.5 4.9 multiply_reduce_fusion.2
  461.7 555.1 %all-gather.33.cloned.1.call-done = bf16[2048,8192]{1,0:T(8,128)(2,1)} async-done(((bf16[512,8192]{1,0:T(8,128)(2,1)}), bf16[2048,8192]{1,0:T(8,128)(2,1)}) %all-gather.33.cloned.1.call-update) | async-done | bytes 33554448 | tf_op jit(solution)/shard_map/all_gather | solution.py:177
  1016.8 21.2 fusion.122
  1038.0 540.0 %all-gather.35.cloned.1.call-done = bf16[2048,8192]{1,0:T(8,128)(2,1)} async-done(((bf16[512,8192]{1,0:T(8,128)(2,1)}), bf16[2048,8192]{1,0:T(8,128)(2,1)}) %all-gather.35.cloned.1.call-update) | async-done | bytes 33554448 | tf_op jit(solution)/shard_map/all_gather | solution.py:178
  1578.0 21.2 fusion.123
  1599.2 540.0 %all-gather.37.cloned.1.call-done = bf16[8192,2048]{1,0:T(8,128)(2,1)} async-done(((bf16[2048,2048]{1,0:T(8,128)(2,1)}), bf16[8192,2048]{1,0:T(8,128)(2,1)}) %all-gather.37.cloned.1.call-update) | async-done | bytes 33554448 | tf_op jit(solution)/shard_map/all_gather | solution.py:179
  2139.2 21.2 multiply_convert_fusion
  2160.4 17.3 fusion.124
  2177.7 18.5 multiply_reduce_fusion
  2198.7 7.3 convolution_convert_fusion.4
  2208.7 35.3 %while.41 = (s32[]{:T(128)}, f32[128,8,4,64]{0,3,2,1:T(8,128)S(1)}, bf16[2,512,8,64]{1,3,2,0:T(8,128)(2,1)}, bf16[2,512,8,64]{1,3,2,0:T(8,128)(2,1)}, bf16[2,512...) while((s32[]{:T(128)}, f32[128,8,4,64]{0,3,2,1:T(8,128)S(1)}, ...), condition=%wide.region_11.12_spmd.clone, body=%wide.region_10.11_spmd.clone.sunk | while | flops 1370030080 | bytes 125557568 | solution.py:261
  2218.3 5.0 fusion.206
  2235.8 5.0 fusion.206
  2261.5 24.3 reduce-scatter.7.cloned.1.call-done
  2287.0 38.6 %reduce-scatter.9.cloned.1.call-done = bf16[128,512]{1,0:T(8,128)(2,1)} async-done(((bf16[1024,512]{1,0:T(8,128)(2,1)}), bf16[128,512]{1,0:T(8,128)(2,1)}) %reduce-scatter.9.cloned.1.call-update) | async-done | bytes 131088
  2334.5 39.4 %all-gather.43.cloned.1.call-done = bf16[512,2048]{0,1:T(8,128)(2,1)} async-done(((bf16[128,2048]{0,1:T(8,128)(2,1)}), bf16[512,2048]{0,1:T(8,128)(2,1)}) %all-gather.43.cloned.1.call-update) | async-done | bytes 2097168 | tf_op jit(solution)/shard_map/all_gather | solution.py:302
  2373.9 46.3 %all-gather.45.cloned.1.call-done = bf16[512,2048]{1,0:T(8,128)(2,1)} async-done(((bf16[128,2048]{1,0:T(8,128)(2,1)}), bf16[512,2048]{1,0:T(8,128)(2,1)}) %all-gather.45.cloned.1.call-update) | async-done | bytes 2097168 | tf_op jit(solution)/shard_map/all_gather | solution.py:303
  2424.6 41.8 %all-gather.39.cloned.1.call-done = bf16[512,2048]{1,0:T(8,128)(2,1)} async-done(((bf16[128,2048]{1,0:T(8,128)(2,1)}), bf16[512,2048]{1,0:T(8,128)(2,1)}) %all-gather.39.cloned.1.call-update) | async-done | bytes 2097168 | tf_op jit(solution)/shard_map/all_gather | solution.py:304
  2466.3 64.2 %all-gather.41.cloned.1.call-done = bf16[512,3072]{0,1:T(8,128)(2,1)} async-done(((bf16[128,3072]{0,1:T(8,128)(2,1)}), bf16[512,3072]{0,1:T(8,128)(2,1)}) %all-gather.41.cloned.1.call-update) | async-done | bytes 3145744 | tf_op jit(solution)/shard_map/all_gather | solution.py:305
  2536.9 39.1 %all-gather.53.cloned.1.call-done = bf16[1,512,2048]{2,1,0:T(8,128)(2,1)} async-done(((bf16[1,128,2048]{2,1,0:T(8,128)(2,1)}), bf16[1,512,2048]{2,1,0:T(8,128)(2,1)}) %all-gather.53.cloned.1.call-update) | async-done | bytes 2097168 | tf_op jit(solution)/shard_map/all_gather | solution.py:213
  2576.1 149.8 %all-gather.51.cloned.1.call-done = bf16[512,8192]{1,0:T(8,128)(2,1)} async-done(((bf16[128,8192]{1,0:T(8,128)(2,1)}), bf16[512,8192]{1,0:T(8,128)(2,1)}) %all-gather.51.cloned.1.call-update) | async-done | bytes 8388624 | tf_op jit(solution)/shard_map/all_gather | solution.py:212
  2725.9 10.1 convolution_convert_fusion.1
  2735.9 35.6 %all-gather.47.cloned.1.call-done = bf16[512,2048]{1,0:T(8,128)(2,1)} async-done(((bf16[128,2048]{1,0:T(8,128)(2,1)}), bf16[512,2048]{1,0:T(8,128)(2,1)}) %all-gather.47.cloned.1.call-update) | async-done | bytes 2097168 | tf_op jit(solution)/shard_map/all_gather | solution.py:214
  2771.5 287.7 %all-gather.49.cloned.1.call-done = bf16[512,16384]{1,0:T(8,128)(2,1)} async-done(((bf16[128,16384]{1,0:T(8,128)(2,1)}), bf16[512,16384]{1,0:T(8,128)(2,1)}) %all-gather.49.cloned.1.call-update) | async-done | bytes 16777232 | tf_op jit(solution)/shard_map/all_gather | solution.py:215
  3059.1 16.0 convolution_convert_fusion
  3075.1 11.8 fusion.118
  3088.9 7.7 fusion.125
  3096.6 17.4 fusion.65
  3116.8 15.6 all-reduce.2
  3132.5 13.1 all-reduce.3
  3149.4 304.3 %all-reduce.7.cloned.1.call-done = (bf16[512,2048]{1,0:T(8,128)(2,1)}, bf16[512,512]{1,0:T(8,128)(2,1)}, bf16[512,512]{1,0:T(8,128)(2,1)}, bf16[512,2048]{1,0:T(...) async-done(((bf16[512,2048]{1,0:T(8,128)(2,1)}, bf16[512,512]{1,0:T(8,128)(2,1)}, bf16[512,512]{1,0:T(8,128)(2,1)}, ...) | async-done | bytes 30408720 | tf_op jit(solution)/shard_map/psum | solution.py:321
  3464.9 11.7 convert_element_type.198
  3476.6 11.7 convert_element_type.199
  3488.3 11.7 convert_element_type.201
  (231 shorter events, 137.4 us)
Async XLA Ops:
  7.2 100.3 %copy-start.5 = (bf16[1,128,2048]{2,1,0:T(8,128)(2,1)S(1)}, bf16[1,128,2048]{2,1,0:T(8,128)(2,1)}, u32[]{:S(2)}) copy-start(bf16[1,128,2048]{2,1,0:T(8,128)(2,1)} %param.18) | copy-start | bytes 1572868
  7.2 51.1 %all-gather.21.cloned.1.call-start = ((), (), s32[]{:S(2)}) async-start(), calls=%async_computation.2 | async-start | bytes 2621440 | tf_op jit(solution)/shard_map/all_gather | solution.py:113
  7.9 96.6 %all-gather.25.cloned.1.call-start = ((), (), s32[]{:S(2)}) async-start(), calls=%async_computation.4 | async-start | bytes 2621440 | tf_op jit(solution)/shard_map/all_gather | solution.py:112
  8.7 120.6 %all-gather.23.cloned.1.call-start = ((), (), s32[]{:S(2)}) async-start(), calls=%async_computation.3 | async-start | bytes 1179648 | tf_op jit(solution)/shard_map/all_gather | solution.py:130
  23.0 295.7 %copy-start.23 = (f32[4,1,512]{2,1,0:T(1,128)}, f32[4,1,512]{2,1,0:T(1,128)S(1)}, u32[]{:S(2)}) copy-start(f32[4,1,512]{2,1,0:T(1,128)S(1)} %convert_element_type.203) | copy-start | bytes 24580
  24.2 294.4 %copy-start.28 = (f32[128]{0:T(128)}, f32[128]{0:T(128)S(1)}, u32[]{:S(2)}) copy-start(f32[128]{0:T(128)S(1)} %add_rsqrt_fusion.1) | copy-start | bytes 1540
  25.5 79.1 %copy-start.13 = (bf16[128,2048]{1,0:T(8,128)(2,1)}, bf16[128,2048]{1,0:T(8,128)(2,1)S(1)}, u32[]{:S(2)}) copy-start(bf16[128,2048]{1,0:T(8,128)(2,1)S(1)} %fusion.74) | copy-start | bytes 1572868
  61.0 94.1 %all-gather.27.cloned.1.call-start = ((), (), s32[]{:S(2)}) async-start(), calls=%async_computation.5 | async-start | bytes 1179648 | tf_op jit(solution)/shard_map/all_gather | solution.py:129
  62.3 262.5 %copy-start.18 = (f32[128,64]{0,1:T(8,128)}, f32[128,64]{0,1:T(8,128)S(1)}, u32[]{:S(2)}) copy-start(f32[128,64]{0,1:T(8,128)S(1)} %pad_maximum_fusion.5) | copy-start | bytes 98308
  62.3 262.5 %copy-start.20 = (f32[128,64]{0,1:T(8,128)}, f32[128,64]{0,1:T(8,128)S(1)}, u32[]{:S(2)}) copy-start(f32[128,64]{0,1:T(8,128)S(1)} %pad_maximum_fusion.4) | copy-start | bytes 98308
  109.0 197.2 %all-gather.29.cloned.1.call-start = ((), (), s32[]{:S(2)}) async-start(), calls=%async_computation.6 | async-start | bytes 10485760 | tf_op jit(solution)/shard_map/all_gather | solution.py:111
  109.6 345.9 %all-gather.31.cloned.1.call-start = ((), (), s32[]{:S(2)}) async-start(), calls=%async_computation.7 | async-start | bytes 10485760 | tf_op jit(solution)/shard_map/all_gather | solution.py:114
  110.2 906.6 %all-gather.33.cloned.1.call-start = ((), (), s32[]{:S(2)}) async-start(), calls=%async_computation.8 | async-start | bytes 41943040 | tf_op jit(solution)/shard_map/all_gather | solution.py:177
  110.9 1467.0 %all-gather.35.cloned.1.call-start = ((), (), s32[]{:S(2)}) async-start(), calls=%async_computation.9 | async-start | bytes 41943040 | tf_op jit(solution)/shard_map/all_gather | solution.py:178
  111.7 2027.5 %all-gather.37.cloned.1.call-start = ((), (), s32[]{:S(2)}) async-start(), calls=%async_computation.10 | async-start | bytes 41943040 | tf_op jit(solution)/shard_map/all_gather | solution.py:179
  112.4 2173.4 %reduce-scatter.7.cloned.1.call-start = ((), (), s32[]{:S(2)}) async-start(), calls=%async_computation.19 | async-start | bytes 1179648
  124.8 2071.5 %copy-start.25 = (f32[4,1,512]{2,1,0:T(1,128)}, f32[4,1,512]{2,1,0:T(1,128)S(1)}, u32[]{:S(2)}) copy-start(f32[4,1,512]{2,1,0:T(1,128)S(1)} %convert_element_type.204) | copy-start | bytes 24580
  460.5 1735.8 %copy-start.30 = (f32[128]{0:T(128)}, f32[128]{0:T(128)S(1)}, u32[]{:S(2)}) copy-start(f32[128]{0:T(128)S(1)} %add_rsqrt_fusion) | copy-start | bytes 1540
  461.7 1116.3 %copy-start.8 = (bf16[128,2048]{1,0:T(8,128)(2,1)}, bf16[128,2048]{1,0:T(8,128)(2,1)S(1)}, u32[]{:S(2)}) copy-start(bf16[128,2048]{1,0:T(8,128)(2,1)S(1)} %multiply_convert_fusion.3) | copy-start | bytes 1572868
  2160.4 17.4 copy-start.3
  2177.7 18.6 copy-start.11
  2196.3 12.4 copy-start.32
  2232.5 8.3 copy-start.16
  2243.9 17.1 copy-start.19
  2251.4 9.9 copy-start.21
  2251.5 74.2 %reduce-scatter.9.cloned.1.call-start = ((), (), s32[]{:S(2)}) async-start(), calls=%async_computation.20 | async-start | bytes 1179648
  2259.1 114.8 %all-gather.43.cloned.1.call-start = ((), (), s32[]{:S(2)}) async-start(), calls=%async_computation.13 | async-start | bytes 2621440 | tf_op jit(solution)/shard_map/all_gather | solution.py:302
  2259.6 160.6 %all-gather.45.cloned.1.call-start = ((), (), s32[]{:S(2)}) async-start(), calls=%async_computation.14 | async-start | bytes 2621440 | tf_op jit(solution)/shard_map/all_gather | solution.py:303
  2260.4 205.9 %all-gather.39.cloned.1.call-start = ((), (), s32[]{:S(2)}) async-start(), calls=%async_computation.11 | async-start | bytes 2621440 | tf_op jit(solution)/shard_map/all_gather | solution.py:304
  2261.0 269.5 %all-gather.41.cloned.1.call-start = ((), (), s32[]{:S(2)}) async-start(), calls=%async_computation.12 | async-start | bytes 3932160 | tf_op jit(solution)/shard_map/all_gather | solution.py:305
  2327.6 248.5 %all-gather.53.cloned.1.call-start = ((), (), s32[]{:S(2)}) async-start(), calls=%async_computation.18 | async-start | bytes 2621440 | tf_op jit(solution)/shard_map/all_gather | solution.py:213
  2328.2 397.7 %all-gather.51.cloned.1.call-start = ((), (), s32[]{:S(2)}) async-start(), calls=%async_computation.17 | async-start | bytes 10485760 | tf_op jit(solution)/shard_map/all_gather | solution.py:212
  2328.8 442.7 %all-gather.47.cloned.1.call-start = ((), (), s32[]{:S(2)}) async-start(), calls=%async_computation.15 | async-start | bytes 2621440 | tf_op jit(solution)/shard_map/all_gather | solution.py:214
  2329.4 729.8 %all-gather.49.cloned.1.call-start = ((), (), s32[]{:S(2)}) async-start(), calls=%async_computation.16 | async-start | bytes 20971520 | tf_op jit(solution)/shard_map/all_gather | solution.py:215
  2334.0 1119.7 %all-reduce.7.cloned.1.call-start = ((), (), s32[]{:S(2)}) async-start(), calls=%async_computation.21 | async-start | bytes 60817408 | tf_op jit(solution)/shard_map/psum | solution.py:321
  3087.0 9.6 copy-start.4
  3096.6 17.4 copy-start.10
  3096.6 18.3 copy-start.6
  3096.6 18.3 copy-start.9
  3096.6 18.3 copy-start.22
  3096.6 18.3 copy-start.24
  3096.6 18.3 copy-start.29
  3114.0 32.7 copy-start.7
  3114.0 32.7 copy-start.12
  3114.0 32.7 copy-start.26
  3114.0 32.7 copy-start.31
  3114.0 32.7 copy-start.33
  3453.7 8.6 copy-start.14
  (13 other events, 45.6 us)
Sparse Core Ops, SparseCore 0:
  9.6 48.6 all-gather.20
  59.8 44.6 all-gather.24
  107.0 22.1 all-gather.22
  131.5 23.5 all-gather.26
  156.5 149.6 all-gather.28
  307.6 147.8 all-gather.30
  457.1 559.6 all-gather.32
  1018.3 559.5 all-gather.34
  1579.5 559.5 all-gather.36
  2251.6 34.1 reduce-scatter.6
  2289.6 35.9 reduce-scatter.8
  2327.6 46.2 all-gather.42
  2376.0 44.1 all-gather.44
  2421.6 44.6 all-gather.38
  2468.3 62.1 all-gather.40
  2531.9 44.1 all-gather.52
  2577.5 148.3 all-gather.50
  2727.3 44.1 all-gather.46
  2773.6 285.4 all-gather.48
  3087.1 366.5 all-reduce.6
where the time goes:
time: 3510 us
  waiting for transfers between devices  3060 us (87%)
  matrix products  235 us (7%)
  other arithmetic  76.8 us (2%)
  local copies, waits for them, and re-layouts  64.8 us (2%)
  blocking collectives  54.3 us (2%)
    all_gather x1, waiting for transfers between devices, on_device(): lax.all_gather(w_gate, 'fsdp', axis=0, tiled=True)  555 us
    all_gather x1, waiting for transfers between devices, on_device(): lax.all_gather(w_down, 'fsdp', axis=0, tiled=True)  540 us
    all_gather x1, waiting for transfers between devices, on_device(): lax.all_gather(w_up, 'fsdp', axis=0, tiled=True)  540 us
    psum x1, waiting for transfers between devices, on_device(): lax.psum(grad_query.astype(jnp.bfloat16), 'ctx').astype(jnp.float32)  304 us
    all_gather x1, waiting for transfers between devices, on_device(): lax.all_gather(gate_up_pair, 'fsdp', axis=0, tiled=True)  288 us
    all_gather x1, waiting for transfers between devices, on_device(): lax.all_gather(hidden, 'fsdp', axis=0, tiled=True)  150 us
    all_gather x1, waiting for transfers between devices, on_device(): lax.all_gather(w_query, 'fsdp', axis=0, tiled=True)  147 us
    all_gather x1, waiting for transfers between devices, on_device(): lax.all_gather(w_out, 'fsdp', axis=0, tiled=True)  98.9 us
  transfers between devices with their start and end apart: 20, of which 20 were waited for; matrix products, arithmetic and copies ran while one was open for 5% of the time, Pallas kernels for 0%

commit v1 on v0

--- a/solution.py
+++ b/solution.py
@@ -318,7 +318,7 @@
     )
     summed = (
         lax.psum(gain_attn_part.astype(jnp.bfloat16), "ctx").astype(jnp.float32),
-        lax.psum(grad_query.astype(jnp.bfloat16), "ctx").astype(jnp.float32),
+        jnp.sum(lax.all_gather(grad_query.astype(jnp.bfloat16), "ctx"), axis=0).astype(jnp.float32),
         lax.psum(grad_key.astype(jnp.bfloat16), "ctx").astype(jnp.float32),
         lax.psum(grad_value.astype(jnp.bfloat16), "ctx").astype(jnp.float32),
         lax.psum(grad_out.astype(jnp.bfloat16), "ctx").astype(jnp.float32),

time: 3510 us -> 3560 us (1.014)
    unnamed x22 -> x23, waiting for transfers between devices: 70.9 us -> 72.1 us
  transfers between devices with their start and end apart: 20 -> 21, of which waited for: 20 -> 20; matrix products, arithmetic and copies ran while one was open for 5% -> 7% of each run, Pallas kernels for 0% -> 0%
where the time goes in v1:
time: 3560 us; the launch traced here: 3550 us
  waiting for transfers between devices  3090 us (87%)
  matrix products  236 us (7%)
  other arithmetic  86.9 us (2%)
  local copies, waits for them, and re-layouts  67.6 us (2%)
  blocking collectives  53.8 us (2%)
    all_gather x1, waiting for transfers between devices, on_device(): lax.all_gather(w_gate, 'fsdp', axis=0, tiled=True)  555 us
    all_gather x1, waiting for transfers between devices, on_device(): lax.all_gather(w_down, 'fsdp', axis=0, tiled=True)  540 us
    all_gather x1, waiting for transfers between devices, on_device(): lax.all_gather(w_up, 'fsdp', axis=0, tiled=True)  540 us
    psum x1, waiting for transfers between devices, on_device(): lax.psum(grad_key.astype(jnp.bfloat16), 'ctx').astype(jnp.float32)  337 us
    all_gather x1, waiting for transfers between devices, on_device(): lax.all_gather(gate_up_pair, 'fsdp', axis=0, tiled=True)  288 us
    all_gather x1, waiting for transfers between devices, on_device(): lax.all_gather(hidden, 'fsdp', axis=0, tiled=True)  150 us
    all_gather x1, waiting for transfers between devices, on_device(): lax.all_gather(w_query, 'fsdp', axis=0, tiled=True)  147 us
    all_gather x1, waiting for transfers between devices, on_device(): lax.all_gather(w_out, 'fsdp', axis=0, tiled=True)  98.9 us
  transfers between devices with their start and end apart: 21, of which 20 were waited for; matrix products, arithmetic and copies ran while one was open for 7% of the time, Pallas kernels for 0%

profile of v1, /device:TPU:0, one launch (start us, length us, event | category | flops | bytes accessed | tf_op | source)
XLA Modules:
  0.0 3550.6 jit_solution(5354227297840074547)
XLA Ops:
  9.4 13.5 all-gather.2
  25.5 32.8 all-gather.23.cloned.1.call-done
  62.3 42.2 %all-gather.27.cloned.1.call-done = bf16[2048,512]{1,0:T(8,128)(2,1)} async-done(((bf16[512,512]{1,0:T(8,128)(2,1)}), bf16[2048,512]{1,0:T(8,128)(2,1)}) %all-gather.27.cloned.1.call-update) | async-done | bytes 2097168 | tf_op jit(solution)/shard_map/all_gather | solution.py:112
  112.6 12.2 all-gather.3
  136.4 18.7 all-gather.29.cloned.1.call-done
  159.2 147.0 %all-gather.31.cloned.1.call-done = bf16[2048,2048]{1,0:T(8,128)(2,1)} async-done(((bf16[512,2048]{1,0:T(8,128)(2,1)}), bf16[2048,2048]{1,0:T(8,128)(2,1)}) %all-gather.31.cloned.1.call-update) | async-done | bytes 8388624 | tf_op jit(solution)/shard_map/all_gather | solution.py:111
  306.2 12.4 copy.73
  318.6 6.0 fusion.98
  324.9 19.0 while.39
  325.1 4.7 fusion.186
  344.0 10.5 while.40
  349.0 5.0 fusion.192
  356.6 98.9 %all-gather.33.cloned.1.call-done = bf16[2048,2048]{1,0:T(8,128)(2,1)} async-done(((bf16[512,2048]{1,0:T(8,128)(2,1)}), bf16[2048,2048]{1,0:T(8,128)(2,1)}) %all-gather.33.cloned.1.call-update) | async-done | bytes 8388624 | tf_op jit(solution)/shard_map/all_gather | solution.py:114
  455.5 4.9 multiply_reduce_fusion.2
  461.7 555.1 %all-gather.35.cloned.1.call-done = bf16[2048,8192]{1,0:T(8,128)(2,1)} async-done(((bf16[512,8192]{1,0:T(8,128)(2,1)}), bf16[2048,8192]{1,0:T(8,128)(2,1)}) %all-gather.35.cloned.1.call-update) | async-done | bytes 33554448 | tf_op jit(solution)/shard_map/all_gather | solution.py:177
  1016.8 21.2 fusion.122
  1038.0 540.0 %all-gather.37.cloned.1.call-done = bf16[2048,8192]{1,0:T(8,128)(2,1)} async-done(((bf16[512,8192]{1,0:T(8,128)(2,1)}), bf16[2048,8192]{1,0:T(8,128)(2,1)}) %all-gather.37.cloned.1.call-update) | async-done | bytes 33554448 | tf_op jit(solution)/shard_map/all_gather | solution.py:178
  1578.0 21.2 fusion.123
  1599.2 540.0 %all-gather.39.cloned.1.call-done = bf16[8192,2048]{1,0:T(8,128)(2,1)} async-done(((bf16[2048,2048]{1,0:T(8,128)(2,1)}), bf16[8192,2048]{1,0:T(8,128)(2,1)}) %all-gather.39.cloned.1.call-update) | async-done | bytes 33554448 | tf_op jit(solution)/shard_map/all_gather | solution.py:179
  2139.2 21.2 multiply_convert_fusion
  2160.4 17.3 fusion.124
  2177.7 18.5 multiply_reduce_fusion
  2198.7 7.3 convolution_convert_fusion.4
  2208.7 35.3 while.41
  2218.3 5.0 fusion.206
  2235.8 5.0 fusion.206
  2260.2 25.6 reduce-scatter.7.cloned.1.call-done
  2287.0 38.6 %reduce-scatter.9.cloned.1.call-done = bf16[128,512]{1,0:T(8,128)(2,1)} async-done(((bf16[1024,512]{1,0:T(8,128)(2,1)}), bf16[128,512]{1,0:T(8,128)(2,1)}) %reduce-scatter.9.cloned.1.call-update) | async-done | bytes 131088
  2335.7 37.3 %all-gather.41.cloned.1.call-done = bf16[512,2048]{1,0:T(8,128)(2,1)} async-done(((bf16[128,2048]{1,0:T(8,128)(2,1)}), bf16[512,2048]{1,0:T(8,128)(2,1)}) %all-gather.41.cloned.1.call-update) | async-done | bytes 2097168 | tf_op jit(solution)/shard_map/all_gather | solution.py:304
  2373.0 64.3 %all-gather.43.cloned.1.call-done = bf16[512,3072]{0,1:T(8,128)(2,1)} async-done(((bf16[128,3072]{0,1:T(8,128)(2,1)}), bf16[512,3072]{0,1:T(8,128)(2,1)}) %all-gather.43.cloned.1.call-update) | async-done | bytes 3145744 | tf_op jit(solution)/shard_map/all_gather | solution.py:305
  2444.5 39.3 %all-gather.45.cloned.1.call-done = bf16[512,2048]{0,1:T(8,128)(2,1)} async-done(((bf16[128,2048]{0,1:T(8,128)(2,1)}), bf16[512,2048]{0,1:T(8,128)(2,1)}) %all-gather.45.cloned.1.call-update) | async-done | bytes 2097168 | tf_op jit(solution)/shard_map/all_gather | solution.py:302
  2483.8 46.2 %all-gather.47.cloned.1.call-done = bf16[512,2048]{1,0:T(8,128)(2,1)} async-done(((bf16[128,2048]{1,0:T(8,128)(2,1)}), bf16[512,2048]{1,0:T(8,128)(2,1)}) %all-gather.47.cloned.1.call-update) | async-done | bytes 2097168 | tf_op jit(solution)/shard_map/all_gather | solution.py:303
  2536.6 39.5 %all-gather.57.cloned.1.call-done = bf16[1,512,2048]{2,1,0:T(8,128)(2,1)} async-done(((bf16[1,128,2048]{2,1,0:T(8,128)(2,1)}), bf16[1,512,2048]{2,1,0:T(8,128)(2,1)}) %all-gather.57.cloned.1.call-update) | async-done | bytes 2097168 | tf_op jit(solution)/shard_map/all_gather | solution.py:213
  2576.1 149.8 %all-gather.53.cloned.1.call-done = bf16[512,8192]{1,0:T(8,128)(2,1)} async-done(((bf16[128,8192]{1,0:T(8,128)(2,1)}), bf16[512,8192]{1,0:T(8,128)(2,1)}) %all-gather.53.cloned.1.call-update) | async-done | bytes 8388624 | tf_op jit(solution)/shard_map/all_gather | solution.py:212
  2725.9 10.1 convolution_convert_fusion.1
  2736.0 35.5 %all-gather.49.cloned.1.call-done = bf16[512,2048]{1,0:T(8,128)(2,1)} async-done(((bf16[128,2048]{1,0:T(8,128)(2,1)}), bf16[512,2048]{1,0:T(8,128)(2,1)}) %all-gather.49.cloned.1.call-update) | async-done | bytes 2097168 | tf_op jit(solution)/shard_map/all_gather | solution.py:214
  2771.5 287.7 %all-gather.51.cloned.1.call-done = bf16[512,16384]{1,0:T(8,128)(2,1)} async-done(((bf16[128,16384]{1,0:T(8,128)(2,1)}), bf16[512,16384]{1,0:T(8,128)(2,1)}) %all-gather.51.cloned.1.call-update) | async-done | bytes 16777232 | tf_op jit(solution)/shard_map/all_gather | solution.py:215
  3059.2 16.0 convolution_convert_fusion
  3075.1 11.8 fusion.118
  3088.9 6.3 fusion.125
  3095.3 19.5 fusion.65
  3117.5 15.7 all-reduce.2
  3133.4 12.4 all-reduce.3
  3149.9 9.5 reduce_sum.90
  3162.5 337.5 %all-reduce.7.cloned.1.call-done = (bf16[512,512]{1,0:T(8,128)(2,1)}, bf16[512,512]{1,0:T(8,128)(2,1)}, bf16[512,2048]{1,0:T(8,128)(2,1)}, bf16[512,8192]{1,0:T(...) async-done(((bf16[512,512]{1,0:T(8,128)(2,1)}, bf16[512,512]{1,0:T(8,128)(2,1)}, bf16[512,2048]{1,0:T(8,128)(2,1)}, bf16[512,8192]{1,0:T(8,128)(2,1)}, ...) | async-done | bytes 28311568 | tf_op jit(solution)/shard_map/psum | solution.py:322
  3508.4 11.7 convert_element_type.200
  3520.1 11.7 convert_element_type.201
  3531.9 11.7 convert_element_type.203
  (235 shorter events, 145.5 us)
Async XLA Ops:
  7.2 100.3 %copy-start.5 = (bf16[1,128,2048]{2,1,0:T(8,128)(2,1)S(1)}, bf16[1,128,2048]{2,1,0:T(8,128)(2,1)}, u32[]{:S(2)}) copy-start(bf16[1,128,2048]{2,1,0:T(8,128)(2,1)} %param.18) | copy-start | bytes 1572868
  7.2 51.1 %all-gather.23.cloned.1.call-start = ((), (), s32[]{:S(2)}) async-start(), calls=%async_computation.2 | async-start | bytes 2621440 | tf_op jit(solution)/shard_map/all_gather | solution.py:113
  7.9 96.6 %all-gather.27.cloned.1.call-start = ((), (), s32[]{:S(2)}) async-start(), calls=%async_computation.4 | async-start | bytes 2621440 | tf_op jit(solution)/shard_map/all_gather | solution.py:112
  8.7 120.6 %all-gather.25.cloned.1.call-start = ((), (), s32[]{:S(2)}) async-start(), calls=%async_computation.3 | async-start | bytes 1179648 | tf_op jit(solution)/shard_map/all_gather | solution.py:130
  23.0 295.7 %copy-start.23 = (f32[4,1,512]{2,1,0:T(1,128)}, f32[4,1,512]{2,1,0:T(1,128)S(1)}, u32[]{:S(2)}) copy-start(f32[4,1,512]{2,1,0:T(1,128)S(1)} %convert_element_type.205) | copy-start | bytes 24580
  24.2 294.4 %copy-start.28 = (f32[128]{0:T(128)}, f32[128]{0:T(128)S(1)}, u32[]{:S(2)}) copy-start(f32[128]{0:T(128)S(1)} %add_rsqrt_fusion.1) | copy-start | bytes 1540
  25.5 79.1 %copy-start.13 = (bf16[128,2048]{1,0:T(8,128)(2,1)}, bf16[128,2048]{1,0:T(8,128)(2,1)S(1)}, u32[]{:S(2)}) copy-start(bf16[128,2048]{1,0:T(8,128)(2,1)S(1)} %fusion.74) | copy-start | bytes 1572868
  61.0 94.1 %all-gather.29.cloned.1.call-start = ((), (), s32[]{:S(2)}) async-start(), calls=%async_computation.5 | async-start | bytes 1179648 | tf_op jit(solution)/shard_map/all_gather | solution.py:129
  62.3 262.5 %copy-start.18 = (f32[128,64]{0,1:T(8,128)}, f32[128,64]{0,1:T(8,128)S(1)}, u32[]{:S(2)}) copy-start(f32[128,64]{0,1:T(8,128)S(1)} %pad_maximum_fusion.5) | copy-start | bytes 98308
  62.3 262.5 %copy-start.20 = (f32[128,64]{0,1:T(8,128)}, f32[128,64]{0,1:T(8,128)S(1)}, u32[]{:S(2)}) copy-start(f32[128,64]{0,1:T(8,128)S(1)} %pad_maximum_fusion.4) | copy-start | bytes 98308
  109.0 197.2 %all-gather.31.cloned.1.call-start = ((), (), s32[]{:S(2)}) async-start(), calls=%async_computation.6 | async-start | bytes 10485760 | tf_op jit(solution)/shard_map/all_gather | solution.py:111
  109.6 345.9 %all-gather.33.cloned.1.call-start = ((), (), s32[]{:S(2)}) async-start(), calls=%async_computation.7 | async-start | bytes 10485760 | tf_op jit(solution)/shard_map/all_gather | solution.py:114
  110.2 906.6 %all-gather.35.cloned.1.call-start = ((), (), s32[]{:S(2)}) async-start(), calls=%async_computation.8 | async-start | bytes 41943040 | tf_op jit(solution)/shard_map/all_gather | solution.py:177
  110.9 1467.0 %all-gather.37.cloned.1.call-start = ((), (), s32[]{:S(2)}) async-start(), calls=%async_computation.9 | async-start | bytes 41943040 | tf_op jit(solution)/shard_map/all_gather | solution.py:178
  111.7 2027.5 %all-gather.39.cloned.1.call-start = ((), (), s32[]{:S(2)}) async-start(), calls=%async_computation.10 | async-start | bytes 41943040 | tf_op jit(solution)/shard_map/all_gather | solution.py:179
  112.4 2173.4 %reduce-scatter.7.cloned.1.call-start = ((), (), s32[]{:S(2)}) async-start(), calls=%async_computation.20 | async-start | bytes 1179648
  124.8 2071.5 %copy-start.25 = (f32[4,1,512]{2,1,0:T(1,128)}, f32[4,1,512]{2,1,0:T(1,128)S(1)}, u32[]{:S(2)}) copy-start(f32[4,1,512]{2,1,0:T(1,128)S(1)} %convert_element_type.206) | copy-start | bytes 24580
  460.5 1735.8 %copy-start.30 = (f32[128]{0:T(128)}, f32[128]{0:T(128)S(1)}, u32[]{:S(2)}) copy-start(f32[128]{0:T(128)S(1)} %add_rsqrt_fusion) | copy-start | bytes 1540
  461.7 1116.3 %copy-start.8 = (bf16[128,2048]{1,0:T(8,128)(2,1)}, bf16[128,2048]{1,0:T(8,128)(2,1)S(1)}, u32[]{:S(2)}) copy-start(bf16[128,2048]{1,0:T(8,128)(2,1)S(1)} %multiply_convert_fusion.3) | copy-start | bytes 1572868
  2160.4 17.4 copy-start.3
  2177.7 18.6 copy-start.11
  2196.3 12.4 copy-start.32
  2232.5 8.3 copy-start.1
  2232.5 8.3 copy-start.16
  2243.9 15.8 copy-start.19
  2251.4 8.6 copy-start.21
  2251.5 74.2 %reduce-scatter.9.cloned.1.call-start = ((), (), s32[]{:S(2)}) async-start(), calls=%async_computation.21 | async-start | bytes 1179648
  2259.1 113.9 %all-gather.41.cloned.1.call-start = ((), (), s32[]{:S(2)}) async-start(), calls=%async_computation.11 | async-start | bytes 2621440 | tf_op jit(solution)/shard_map/all_gather | solution.py:304
  2259.6 177.7 %all-gather.43.cloned.1.call-start = ((), (), s32[]{:S(2)}) async-start(), calls=%async_computation.12 | async-start | bytes 3932160 | tf_op jit(solution)/shard_map/all_gather | solution.py:305
  2327.6 156.1 %all-gather.45.cloned.1.call-start = ((), (), s32[]{:S(2)}) async-start(), calls=%async_computation.13 | async-start | bytes 2621440 | tf_op jit(solution)/shard_map/all_gather | solution.py:302
  2328.2 201.8 %all-gather.47.cloned.1.call-start = ((), (), s32[]{:S(2)}) async-start(), calls=%async_computation.14 | async-start | bytes 2621440 | tf_op jit(solution)/shard_map/all_gather | solution.py:303
  2328.8 247.3 %all-gather.57.cloned.1.call-start = ((), (), s32[]{:S(2)}) async-start(), calls=%async_computation.19 | async-start | bytes 2621440 | tf_op jit(solution)/shard_map/all_gather | solution.py:213
  2329.4 396.5 %all-gather.53.cloned.1.call-start = ((), (), s32[]{:S(2)}) async-start(), calls=%async_computation.17 | async-start | bytes 10485760 | tf_op jit(solution)/shard_map/all_gather | solution.py:212
  2329.9 441.5 %all-gather.49.cloned.1.call-start = ((), (), s32[]{:S(2)}) async-start(), calls=%async_computation.15 | async-start | bytes 2621440 | tf_op jit(solution)/shard_map/all_gather | solution.py:214
  2330.5 728.6 %all-gather.51.cloned.1.call-start = ((), (), s32[]{:S(2)}) async-start(), calls=%async_computation.16 | async-start | bytes 20971520 | tf_op jit(solution)/shard_map/all_gather | solution.py:215
  2335.2 814.7 %all-gather.55.cloned.1.call-start = ((), (), s32[]{:S(2)}) async-start(), calls=%async_computation.18 | async-start | bytes 18874368 | tf_op jit(solution)/shard_map/all_gather | solution.py:321
  2444.4 1055.5 %all-reduce.7.cloned.1.call-start = ((), (), s32[]{:S(2)}) async-start(), calls=%async_computation.22 | async-start | bytes 56623104 | tf_op jit(solution)/shard_map/psum | solution.py:322
  3095.2 19.5 copy-start.10
  3095.2 20.4 copy-start.6
  3095.2 20.4 copy-start.9
  3095.2 20.4 copy-start.22
  3095.2 20.4 copy-start.24
  3095.2 20.4 copy-start.29
  3114.7 32.3 copy-start.7
  3114.7 32.3 copy-start.12
  3114.7 32.3 copy-start.26
  3114.8 32.2 copy-start.31
  3114.8 32.2 copy-start.33
  (14 other events, 47.1 us)
Sparse Core Ops, SparseCore 0:
  9.6 48.6 all-gather.22
  59.8 44.6 all-gather.26
  107.0 22.1 all-gather.24
  131.5 23.5 all-gather.28
  156.5 149.6 all-gather.30
  307.6 147.8 all-gather.32
  457.1 559.6 all-gather.34
  1018.3 559.5 all-gather.36
  1579.5 559.5 all-gather.38
  2251.6 34.1 reduce-scatter.6
  2289.6 35.9 reduce-scatter.8
  2327.0 45.9 all-gather.40
  2375.1 62.1 all-gather.42
  2439.3 44.4 all-gather.44
  2485.7 44.1 all-gather.46
  2531.4 44.6 all-gather.56
  2577.5 148.3 all-gather.52
  2727.3 44.1 all-gather.48
  2773.6 285.4 all-gather.50
  3060.9 88.2 all-gather.54
  3155.2 344.7 all-reduce.6
